TPU v7x, 256 devices: a whole 4x4x8 slice. The times are simulated.
256 devices in a mesh: dp: 16 (over z, x_lo), tensor: 16 (over y, x_hi, core).
Axes of the slice: x: 4 (x_hi: 2, x_lo: 2; x = x_hi * 2 + x_lo), y: 4, z: 8, core: 2. Of those that a mesh axis runs over, the one named last changes fastest.
Arguments:
- activations: bfloat16 [8192, 32768], P('tensor', 'dp'), may hold values from -6 to 6
- cotangent: bfloat16 [8192, 32768], P('tensor', 'dp'), may hold values from -6 to 6
- first_up: bfloat16 [64, 128, 128], P('tensor', 'dp'), may hold values from -0.5 to 0.5
- second_up: bfloat16 [128, 64, 256], P('tensor', 'dp'), may hold values from -0.75 to 0.75
- second_down: bfloat16 [128, 64, 256], P('tensor', 'dp'), may hold values from -0.375 to 0.375
- first_down: bfloat16 [64, 128, 128], P('tensor', 'dp'), may hold values from -0.5 to 0.5
Outputs:
- output: bfloat16 [8192, 32768], P('tensor', 'dp')
- grad_input: bfloat16 [8192, 32768], P('tensor', 'dp')
- grad_first_up: float32 [64, 128, 128], P('tensor', 'dp')
- grad_second_up: float32 [128, 64, 256], P('tensor', 'dp')
- grad_second_down: float32 [128, 64, 256], P('tensor', 'dp')
- grad_first_down: float32 [64, 128, 128], P('tensor', 'dp')
All inputs are finite; a program needn't handle non-finite values.
Results may differ from a plain program's by a relative error of at most 0.007.
Values may be sent and summed in bfloat16 or wider, within the bound.
A program may use at most 128 MiB of HBM per device.

v0:
```python
import jax
import jax.numpy as jnp
from jax import lax
from jax.sharding import PartitionSpec as P


def gelu_value(v):
    return 0.5 * v * (1.0 + lax.erf(v * 0.7071067811865476))


def gelu_slope(v):
    return (
        0.5 * (1.0 + lax.erf(v * 0.7071067811865476))
        + v * jnp.exp(-0.5 * v * v) * 0.3989422804014327
    )


def product(form, left, right):
    return jnp.einsum(form, left, right, preferred_element_type=jnp.float32)


def transpose_blocks(values):
    return lax.all_to_all(values, "tensor", split_axis=1, concat_axis=0, tiled=True)


def restore_blocks(values):
    return lax.all_to_all(values, "tensor", split_axis=0, concat_axis=1, tiled=True)


def local(activations, cotangent, first_up, second_up, second_down, first_down):
    width_local, tokens = activations.shape
    blocks_local = first_up.shape[0]
    block_size = first_up.shape[2]
    inputs = activations.reshape(blocks_local, block_size, tokens)
    grads_in = cotangent.reshape(blocks_local, block_size, tokens)
    up_one, up_two, down_two, down_one = (
        lax.all_gather(first_up, "dp", axis=1, tiled=True),
        lax.all_gather(second_up, "dp", axis=1, tiled=True),
        lax.all_gather(second_down, "dp", axis=1, tiled=True),
        lax.all_gather(first_down, "dp", axis=1, tiled=True),
    )
    section_one = product("kit,kij->kjt", inputs, up_one).astype(jnp.bfloat16)
    moved_one = transpose_blocks(section_one)
    pre = product("kjt,jkm->jmt", moved_one, up_two)
    hid = gelu_value(pre).astype(jnp.bfloat16)
    section_three = product("jmt,jkm->kjt", hid, down_two).astype(jnp.bfloat16)
    moved_three = restore_blocks(section_three)
    result = product("kjt,kji->kit", moved_three, down_one).astype(jnp.bfloat16)
    part_r2 = product("kjt,kit->kji", moved_three, grads_in)
    back_three = product("kit,kji->kjt", grads_in, down_one).astype(jnp.bfloat16)
    moved_back = transpose_blocks(back_three)
    part_l2 = product("jmt,kjt->jkm", hid, moved_back)
    back_hid = product("kjt,jkm->jmt", moved_back, down_two)
    back_pre = (back_hid * gelu_slope(pre)).astype(jnp.bfloat16)
    part_l1 = product("kjt,jmt->jkm", moved_one, back_pre)
    back_one = product("jmt,jkm->kjt", back_pre, up_two).astype(jnp.bfloat16)
    local_back = restore_blocks(back_one)
    part_r1 = product("kit,kjt->kij", inputs, local_back)
    grad_in = product("kjt,kij->kit", local_back, up_one).astype(jnp.bfloat16)
    sum_r1, sum_l1, sum_l2, sum_r2 = (
        lax.psum_scatter(part_r1, "dp", scatter_dimension=1, tiled=True),
        lax.psum_scatter(part_l1, "dp", scatter_dimension=1, tiled=True),
        lax.psum_scatter(part_l2, "dp", scatter_dimension=1, tiled=True),
        lax.psum_scatter(part_r2, "dp", scatter_dimension=1, tiled=True),
    )
    output = result.reshape(width_local, tokens)
    grad_input = grad_in.reshape(width_local, tokens)
    return (output, grad_input, sum_r1, sum_l1, sum_l2, sum_r2)


def solution(mesh):
    in_specs = (
        P("tensor", "dp"),
        P("tensor", "dp"),
        P("tensor", "dp", None),
        P("tensor", "dp", None),
        P("tensor", "dp", None),
        P("tensor", "dp", None),
    )
    out_specs = (
        P("tensor", "dp"),
        P("tensor", "dp"),
        P("tensor", "dp", None),
        P("tensor", "dp", None),
        P("tensor", "dp", None),
        P("tensor", "dp", None),
    )
    return jax.shard_map(local, mesh=mesh, in_specs=in_specs, out_specs=out_specs, check_vma=False)
```

profile of v0, /device:TPU:8, one launch (start us, length us, event | category | flops | bytes accessed | tf_op | source)
XLA Modules:
  0.0 613.0 jit_solution(7144741162166313327)
XLA Ops:
  7.2 37.4 %all_gather.12 = bf16[4,128,128]{2,1,0:T(8,128)(2,1)S(1)} all-gather(bf16[4,8,128]{2,1,0:T(8,128)(2,1)} %param.8), channel_id=1, replica_groups=mesh['dp'=16,'tensor'=16] {'dp'}, dimensions={1}, use_global_device_ids=true | all-gather | bytes 139264 | tf_op jit(solution)/shard_map/all_gather | solution.py:37
  45.3 2.9 copy.21
  48.3 7.2 %all-to-all-start = ((bf16[4,128,2048]{2,0,1:T(4,128)(2,1)}), bf16[4,128,2048]{2,0,1:T(4,128)(2,1)}, u32[]{:S(2)}, u32[]{:S(2)}) async-start(bf16[4,128,2048]{2,0,1:T(4,128)(2,1)} %copy.21), calls=%async_computation | async-start | bytes 4194304 | tf_op jit(solution)/shard_map/all_to_all | solution.py:23
  55.5 50.0 %all_gather.15 = bf16[4,128,128]{2,1,0:T(8,128)(2,1)S(1)} all-gather(bf16[4,8,128]{2,1,0:T(8,128)(2,1)S(1)} %copy-done.5), channel_id=1, replica_groups=mesh['dp'=16,'tensor'=16] {'dp'}, dimensions={1}, use_global_device_ids=true | all-gather | bytes 139264 | tf_op jit(solution)/shard_map/all_gather | solution.py:40
  105.5 2.3 convolution_convert_fusion.3
  107.8 3.0 copy.30
  110.8 7.2 %all-to-all-start.2 = ((bf16[4,128,2048]{2,0,1:T(4,128)(2,1)}), bf16[4,128,2048]{2,0,1:T(4,128)(2,1)}, u32[]{:S(2)}, u32[]{:S(2)}) async-start(bf16[4,128,2048]{2,0,1:T(4,128)(2,1)} %copy.30), calls=%async_computation.2 | async-start | bytes 4194304 | tf_op jit(solution)/shard_map/all_to_all | solution.py:23
  118.0 51.3 %all_gather.13 = bf16[8,64,256]{2,0,1:T(8,128)(2,1)S(1)} all-gather(bf16[8,4,256]{2,0,1:T(8,128)(2,1)S(1)} %copy.23), channel_id=1, replica_groups=mesh['dp'=16,'tensor'=16] {'dp'}, dimensions={1}, use_global_device_ids=true | all-gather | bytes 278528 | tf_op jit(solution)/shard_map/all_gather | solution.py:38
  169.3 31.1 %all_gather.14 = bf16[8,64,256]{2,0,1:T(8,128)(2,1)S(1)} all-gather(bf16[8,4,256]{2,0,1:T(8,128)(2,1)S(1)} %copy.25), channel_id=1, replica_groups=mesh['dp'=16,'tensor'=16] {'dp'}, dimensions={1}, use_global_device_ids=true | all-gather | bytes 278528 | tf_op jit(solution)/shard_map/all_gather | solution.py:39
  200.4 4.3 copy.80
  204.7 3.9 all_to_all.55
  208.6 4.3 copy.79
  212.9 4.0 all_to_all.63
  216.9 7.5 %fusion.7 = (bf16[8,256,2048]{1,2,0:T(8,128)(2,1)}, f32[8,2048,256]{2,1,0:T(8,128)S(1)}) fusion(bf16[64,8,2048]{2,0,1:T(8,128)(2,1)} %all_to_all.55, bf16[8,64,256]{2,0,1:T(8,128)(2,1)S(1)} %all_gather.13), kind=kOutput, calls=%fused_computation.10 | convolution fusion | flops 557842432 | bytes 27525120 | tf_op jit(solution)/shard_map/kjt,jkm->jmt/dot_general | solution.py:19
  224.4 8.5 %fusion.5 = bf16[8,256,2048]{1,2,0:T(8,128)(2,1)S(1)} fusion(f32[8,2048,256]{2,1,0:T(8,128)S(1)} %get-tuple-element.19, bf16[64,8,2048]{2,0,1:T(8,128)(2,1)S(1)} %copy-done.2, bf16[8,64,256]{2,0,1:T(8,128)(2,1)S(1)} %all_gather.14), kind=kOutput, calls=%fused_computation.6 | convolution fusion | flops 578813952 | bytes 27525120 | tf_op jit(solution)/shard_map/kjt,jkm->jmt/dot_general | solution.py:19
  232.9 2.6 fusion.11
  236.1 2.5 copy.35
  238.6 7.3 %all-to-all-start.3 = ((bf16[64,8,2048]{2,1,0:T(8,128)(2,1)}), bf16[64,8,2048]{2,1,0:T(8,128)(2,1)}, u32[]{:S(2)}, u32[]{:S(2)}) async-start(bf16[64,8,2048]{2,1,0:T(8,128)(2,1)} %copy.35), calls=%async_computation.3 | async-start | bytes 4194304 | tf_op jit(solution)/shard_map/all_to_all | solution.py:27
  245.9 5.5 fusion.30
  252.5 6.0 fusion.10
  258.5 2.5 copy.28
  261.0 13.4 %all-to-all-done.3 = bf16[64,8,2048]{2,1,0:T(8,128)(2,1)} async-done(((bf16[64,8,2048]{2,1,0:T(8,128)(2,1)}), bf16[64,8,2048]{2,1,0:T(8,128)(2,1)}, u32[]{:S(2)}, u32[]{:S(2)}) %all-to-all-start.3) | async-done | bytes 2097184 | tf_op jit(solution)/shard_map/all_to_all | solution.py:27
  274.4 6.5 %all-to-all-start.1 = ((bf16[64,8,2048]{2,1,0:T(8,128)(2,1)}), bf16[64,8,2048]{2,1,0:T(8,128)(2,1)}, u32[]{:S(2)}, u32[]{:S(2)}) async-start(bf16[64,8,2048]{2,1,0:T(8,128)(2,1)} %copy.28), calls=%async_computation.1 | async-start | bytes 4194304 | tf_op jit(solution)/shard_map/all_to_all | solution.py:27
  281.2 5.5 fusion.31
  289.1 34.2 %reduce-scatter.4.cloned.1.call-done = f32[8,4,256]{2,0,1:T(8,128)} async-done(((f32[8,64,256]{2,0,1:T(8,128)}), f32[8,4,256]{2,0,1:T(8,128)}) %reduce-scatter.4.cloned.1.call-update) | async-done | bytes 32784 | tf_op jit(solution)/shard_map/reduce_scatter | solution.py:62
  324.7 70.0 %reduce-scatter.6.cloned.1.call-done = f32[8,4,256]{2,0,1:T(8,128)} async-done(((f32[8,64,256]{2,0,1:T(8,128)}), f32[8,4,256]{2,0,1:T(8,128)}) %reduce-scatter.6.cloned.1.call-update) | async-done | bytes 32784 | tf_op jit(solution)/shard_map/reduce_scatter | solution.py:63
  396.1 2.3 fusion.22
  399.3 3.6 fusion.12
  402.9 3.6 convolution_convert_fusion.2
  406.6 3.7 convolution_convert_fusion.4
  410.2 123.3 %all-reduce.3.cloned.1.call-done = f32[4,128,128]{2,0,1:T(4,128)} async-done(((f32[4,128,128]{2,0,1:T(4,128)}), f32[4,128,128]{2,0,1:T(4,128)}) %all-reduce.3.cloned.1.call-update) | async-done | bytes 262160
  534.8 71.7 %reduce-scatter.8.cloned.1.call-done = f32[4,8,128]{2,1,0:T(8,128)} async-done(((f32[4,128,128]{2,1,0:T(8,128)}), f32[4,8,128]{2,1,0:T(8,128)}) %reduce-scatter.8.cloned.1.call-update) | async-done | bytes 16400 | tf_op jit(solution)/shard_map/reduce_scatter | solution.py:64
  (36 shorter events, 9.6 us)
Async XLA Ops:
  7.2 37.4 %copy-start = (bf16[512,2048]{1,0:T(8,128)(2,1)S(1)}, bf16[512,2048]{1,0:T(8,128)(2,1)}, u32[]{:S(2)}) copy-start(bf16[512,2048]{1,0:T(8,128)(2,1)} %param.6) | copy-start | bytes 6291460
  48.3 7.2 %copy-start.5 = (bf16[4,8,128]{2,1,0:T(8,128)(2,1)S(1)}, bf16[4,8,128]{2,1,0:T(8,128)(2,1)}, u32[]{:S(2)}) copy-start(bf16[4,8,128]{2,1,0:T(8,128)(2,1)} %param.11) | copy-start | bytes 24580
  48.3 62.5 %all-to-all-start = ((bf16[4,128,2048]{2,0,1:T(4,128)(2,1)}), bf16[4,128,2048]{2,0,1:T(4,128)(2,1)}, u32[]{:S(2)}, u32[]{:S(2)}) async-start(bf16[4,128,2048]{2,0,1:T(4,128)(2,1)} %copy.21), calls=%async_computation | async-start | bytes 4194304 | tf_op jit(solution)/shard_map/all_to_all | solution.py:23
  110.8 7.2 %copy-start.3 = (bf16[8,4,256]{2,1,0:T(4,128)(2,1)S(1)}, bf16[8,4,256]{2,1,0:T(4,128)(2,1)}, u32[]{:S(2)}) copy-start(bf16[8,4,256]{2,1,0:T(4,128)(2,1)} %param.9) | copy-start | bytes 49156
  110.8 7.2 %copy-start.4 = (bf16[8,4,256]{2,1,0:T(4,128)(2,1)S(1)}, bf16[8,4,256]{2,1,0:T(4,128)(2,1)}, u32[]{:S(2)}) copy-start(bf16[8,4,256]{2,1,0:T(4,128)(2,1)} %param.10) | copy-start | bytes 49156
  110.8 97.8 %all-to-all-start.2 = ((bf16[4,128,2048]{2,0,1:T(4,128)(2,1)}), bf16[4,128,2048]{2,0,1:T(4,128)(2,1)}, u32[]{:S(2)}, u32[]{:S(2)}) async-start(bf16[4,128,2048]{2,0,1:T(4,128)(2,1)} %copy.30), calls=%async_computation.2 | async-start | bytes 4194304 | tf_op jit(solution)/shard_map/all_to_all | solution.py:23
  216.9 7.5 %copy-start.2 = (bf16[64,8,2048]{2,0,1:T(8,128)(2,1)S(1)}, bf16[64,8,2048]{2,0,1:T(8,128)(2,1)}, u32[]{:S(2)}) copy-start(bf16[64,8,2048]{2,0,1:T(8,128)(2,1)} %all_to_all.63) | copy-start | bytes 6291460
  232.8 3.2 copy-start.1
  238.6 35.8 %all-to-all-start.3 = ((bf16[64,8,2048]{2,1,0:T(8,128)(2,1)}), bf16[64,8,2048]{2,1,0:T(8,128)(2,1)}, u32[]{:S(2)}, u32[]{:S(2)}) async-start(bf16[64,8,2048]{2,1,0:T(8,128)(2,1)} %copy.35), calls=%async_computation.3 | async-start | bytes 4194304 | tf_op jit(solution)/shard_map/all_to_all | solution.py:27
  245.9 77.5 %reduce-scatter.4.cloned.1.call-start = ((), (), s32[]{:S(2)}) async-start(), calls=%async_computation.7 | async-start | bytes 557056 | tf_op jit(solution)/shard_map/reduce_scatter | solution.py:62
  274.4 124.9 %all-to-all-start.1 = ((bf16[64,8,2048]{2,1,0:T(8,128)(2,1)}), bf16[64,8,2048]{2,1,0:T(8,128)(2,1)}, u32[]{:S(2)}, u32[]{:S(2)}) async-start(bf16[64,8,2048]{2,1,0:T(8,128)(2,1)} %copy.28), calls=%async_computation.1 | async-start | bytes 4194304 | tf_op jit(solution)/shard_map/all_to_all | solution.py:27
  280.9 6.9 %copy-start.6 = (u32[256]{0:T(256)S(1)}, u32[256]{0:T(256)}, u32[]{:S(2)}) copy-start(u32[256]{0:T(256)} %constant.16) | copy-start | bytes 3076
  280.9 113.8 %reduce-scatter.6.cloned.1.call-start = ((), (), s32[]{:S(2)}) async-start(), calls=%async_computation.8 | async-start | bytes 557056 | tf_op jit(solution)/shard_map/reduce_scatter | solution.py:63
  287.8 245.7 %all-reduce.3.cloned.1.call-start = ((), (), s32[]{:S(2)}) async-start(), calls=%async_computation.10 | async-start | bytes 524288
  399.2 207.3 %reduce-scatter.8.cloned.1.call-start = ((), (), s32[]{:S(2)}) async-start(), calls=%async_computation.9 | async-start | bytes 278528 | tf_op jit(solution)/shard_map/reduce_scatter | solution.py:64
Sparse Core Ops, SparseCore 0:
  252.6 70.6 reduce-scatter.3
  326.0 68.6 reduce-scatter.5
  399.4 134.1 all-reduce.2
  536.6 69.8 reduce-scatter.7
where the time goes:
time: 614 us; the launch traced here: 613 us
  waiting for transfers between devices  313 us (51%)
  blocking collectives  170 us (28%)
  matrix products  51.8 us (8%)
  local copies, waits for them, and re-layouts  35.7 us (6%)
  starting transfers between devices  28.6 us (5%)
  between operations  14.5 us (2%)
    unnamed x5, waiting for transfers between devices  123 us
    reduce_scatter x1, waiting for transfers between devices, local(): lax.psum_scatter(part_r2, 'dp', scatter_dimension=1, tiled=True)  71.7 us
    reduce_scatter x1, waiting for transfers between devices, local(): lax.psum_scatter(part_l2, 'dp', scatter_dimension=1, tiled=True)  70 us
    dot_general x12, matrix products, product(): return jnp.einsum(form, left, right, preferred_element_type=jnp.float32)  51.8 us
    all_gather x1, blocking collectives, local(): lax.all_gather(second_up, 'dp', axis=1, tiled=True)  51.3 us
    all_gather x1, blocking collectives, local(): lax.all_gather(first_down, 'dp', axis=1, tiled=True)  50 us
    all_gather x1, blocking collectives, local(): lax.all_gather(first_up, 'dp', axis=1, tiled=True)  37.4 us
    reduce_scatter x1, waiting for transfers between devices, local(): lax.psum_scatter(part_l1, 'dp', scatter_dimension=1, tiled=True)  34.2 us
  transfers between devices with their start and end apart: 8, of which 5 were waited for; matrix products, arithmetic and copies ran while one was open for 8% of the time, Pallas kernels for 0%

commit v1 on v0

--- a/solution.py
+++ b/solution.py
@@ -36,7 +36,9 @@
     up_one, up_two, down_two, down_one = (
         lax.all_gather(first_up, "dp", axis=1, tiled=True),
         lax.all_gather(second_up, "dp", axis=1, tiled=True),
-        lax.all_gather(second_down, "dp", axis=1, tiled=True),
+        jnp.concatenate(
+            lax.all_to_all(jnp.stack([second_down] * lax.axis_size("dp")), "dp", 0, 0), axis=1
+        ),
         lax.all_gather(first_down, "dp", axis=1, tiled=True),
     )
     section_one = product("kit,kij->kjt", inputs, up_one).astype(jnp.bfloat16)

time: 614 us -> 592 us (0.964)
  blocking collectives: 170 us -> 136 us
  starting transfers between devices: 28.6 us -> 38 us
    all_gather x1 -> x0, blocking collectives: 31.1 us -> none  [local(): lax.all_gather(second_down, 'dp', axis=1, tiled=True)]
    all_to_all x0 -> x1, starting transfers between devices: none -> 9.5 us  [local(): lax.all_to_all(jnp.stack([second_down] * lax.axis_size('dp')), 'dp', 0, 0)]
  transfers between devices with their start and end apart: 8 -> 9, of which waited for: 5 -> 5; matrix products, arithmetic and copies ran while one was open for 8% -> 9% of each run, Pallas kernels for 0% -> 0%
where the time goes in v1:
time: 592 us; the launch traced here: 591 us
  waiting for transfers between devices  314 us (53%)
  blocking collectives  136 us (23%)
  matrix products  51.8 us (9%)
  starting transfers between devices  38 us (6%)
  local copies, waits for them, and re-layouts  37.5 us (6%)
  between operations  14.6 us (2%)
    unnamed x5, waiting for transfers between devices  123 us
    reduce_scatter x1, waiting for transfers between devices, local(): lax.psum_scatter(part_r2, 'dp', scatter_dimension=1, tiled=True)  71.7 us
    reduce_scatter x1, waiting for transfers between devices, local(): lax.psum_scatter(part_l2, 'dp', scatter_dimension=1, tiled=True)  69.8 us
    dot_general x12, matrix products, product(): return jnp.einsum(form, left, right, preferred_element_type=jnp.float32)  51.8 us
    all_gather x1, blocking collectives, local(): lax.all_gather(second_up, 'dp', axis=1, tiled=True)  51 us
    all_gather x1, blocking collectives, local(): lax.all_gather(first_down, 'dp', axis=1, tiled=True)  50 us
    reduce_scatter x1, waiting for transfers between devices, local(): lax.psum_scatter(part_l1, 'dp', scatter_dimension=1, tiled=True)  35.5 us
    all_gather x1, blocking collectives, local(): lax.all_gather(first_up, 'dp', axis=1, tiled=True)  34.6 us
  transfers between devices with their start and end apart: 9, of which 5 were waited for; matrix products, arithmetic and copies ran while one was open for 9% of the time, Pallas kernels for 0%

profile of v1, /device:TPU:8, one launch (start us, length us, event | category | flops | bytes accessed | tf_op | source)
XLA Modules:
  0.0 590.9 jit_solution(4069069784914590738)
XLA Ops:
  8.9 9.5 %all-to-all-start.1 = ((bf16[16,8,4,256]{3,2,1,0:T(4,128)(2,1)}), bf16[16,8,4,256]{3,2,1,0:T(4,128)(2,1)S(1)}, u32[]{:S(2)}, u32[]{:S(2)}) async-start(bf16[16,8,4,256]{3,2,1,0:T(4,128)(2,1)} %stack.2), calls=%async_computation.1 | async-start | bytes 524288 | tf_op jit(solution)/shard_map/all_to_all | solution.py:40
  18.4 34.6 %all_gather.9 = bf16[4,128,128]{2,1,0:T(8,128)(2,1)S(1)} all-gather(bf16[4,8,128]{2,1,0:T(8,128)(2,1)} %param.8), channel_id=1, replica_groups=mesh['dp'=16,'tensor'=16] {'dp'}, dimensions={1}, use_global_device_ids=true | all-gather | bytes 139264 | tf_op jit(solution)/shard_map/all_gather | solution.py:37
  53.7 2.9 copy.21
  56.6 7.2 %all-to-all-start = ((bf16[4,128,2048]{2,0,1:T(4,128)(2,1)}), bf16[4,128,2048]{2,0,1:T(4,128)(2,1)}, u32[]{:S(2)}, u32[]{:S(2)}) async-start(bf16[4,128,2048]{2,0,1:T(4,128)(2,1)} %copy.21), calls=%async_computation | async-start | bytes 4194304 | tf_op jit(solution)/shard_map/all_to_all | solution.py:23
  63.9 50.0 %all_gather.11 = bf16[4,128,128]{2,1,0:T(8,128)(2,1)S(1)} all-gather(bf16[4,8,128]{2,1,0:T(8,128)(2,1)S(1)} %copy-done.4), channel_id=1, replica_groups=mesh['dp'=16,'tensor'=16] {'dp'}, dimensions={1}, use_global_device_ids=true | all-gather | bytes 139264 | tf_op jit(solution)/shard_map/all_gather | solution.py:42
  113.9 2.3 convolution_convert_fusion.3
  116.2 3.0 copy.29
  119.2 7.2 %all-to-all-start.3 = ((bf16[4,128,2048]{2,0,1:T(4,128)(2,1)}), bf16[4,128,2048]{2,0,1:T(4,128)(2,1)}, u32[]{:S(2)}, u32[]{:S(2)}) async-start(bf16[4,128,2048]{2,0,1:T(4,128)(2,1)} %copy.29), calls=%async_computation.3 | async-start | bytes 4194304 | tf_op jit(solution)/shard_map/all_to_all | solution.py:23
  126.4 51.0 %all_gather.10 = bf16[8,64,256]{2,0,1:T(8,128)(2,1)S(1)} all-gather(bf16[8,4,256]{2,0,1:T(8,128)(2,1)S(1)} %copy.23), channel_id=1, replica_groups=mesh['dp'=16,'tensor'=16] {'dp'}, dimensions={1}, use_global_device_ids=true | all-gather | bytes 278528 | tf_op jit(solution)/shard_map/all_gather | solution.py:38
  177.5 4.3 copy.74
  181.8 3.9 all_to_all.58
  185.7 4.3 copy.73
  190.0 4.0 all_to_all.67
  193.9 7.5 %fusion.7 = (bf16[8,256,2048]{1,2,0:T(8,128)(2,1)}, f32[8,2048,256]{2,1,0:T(8,128)S(1)}) fusion(bf16[64,8,2048]{2,0,1:T(8,128)(2,1)} %all_to_all.58, bf16[8,64,256]{2,0,1:T(8,128)(2,1)S(1)} %all_gather.10), kind=kOutput, calls=%fused_computation.10 | convolution fusion | flops 557842432 | bytes 27525120 | tf_op jit(solution)/shard_map/kjt,jkm->jmt/dot_general | solution.py:19
  201.4 8.5 %fusion.5 = bf16[8,256,2048]{1,2,0:T(8,128)(2,1)S(1)} fusion(f32[8,2048,256]{2,1,0:T(8,128)S(1)} %get-tuple-element.19, bf16[64,8,2048]{2,0,1:T(8,128)(2,1)S(1)} %copy-done.2, bf16[8,64,256]{2,1,0:T(8,128)(2,1)S(1)} %reshape.34), kind=kOutput, calls=%fused_computation.6 | convolution fusion | flops 578813952 | bytes 27525120 | tf_op jit(solution)/shard_map/kjt,jkm->jmt/dot_general | solution.py:19
  209.9 2.6 fusion.11
  213.2 2.5 copy.33
  215.7 7.2 %all-to-all-start.4 = ((bf16[64,8,2048]{2,1,0:T(8,128)(2,1)}), bf16[64,8,2048]{2,1,0:T(8,128)(2,1)}, u32[]{:S(2)}, u32[]{:S(2)}) async-start(bf16[64,8,2048]{2,1,0:T(8,128)(2,1)} %copy.33), calls=%async_computation.4 | async-start | bytes 4194304 | tf_op jit(solution)/shard_map/all_to_all | solution.py:27
  222.9 5.5 fusion.28
  229.5 6.0 %fusion.10 = bf16[64,8,2048]{2,0,1:T(8,128)(2,1)S(1)} fusion(bf16[8,256,2048]{1,2,0:T(8,128)(2,1)} %get-tuple-element.18, bf16[8,64,256]{2,1,0:T(8,128)(2,1)S(1)} %reshape.34), kind=kOutput, calls=%fused_computation.19 | convolution fusion | flops 537919488 | bytes 10747904 | tf_op jit(solution)/shard_map/jmt,jkm->kjt/dot_general | solution.py:19
  235.5 2.5 copy.27
  238.0 13.2 %all-to-all-done.4 = bf16[64,8,2048]{2,1,0:T(8,128)(2,1)} async-done(((bf16[64,8,2048]{2,1,0:T(8,128)(2,1)}), bf16[64,8,2048]{2,1,0:T(8,128)(2,1)}, u32[]{:S(2)}, u32[]{:S(2)}) %all-to-all-start.4) | async-done | bytes 2097184 | tf_op jit(solution)/shard_map/all_to_all | solution.py:27
  251.1 6.5 %all-to-all-start.2 = ((bf16[64,8,2048]{2,1,0:T(8,128)(2,1)}), bf16[64,8,2048]{2,1,0:T(8,128)(2,1)}, u32[]{:S(2)}, u32[]{:S(2)}) async-start(bf16[64,8,2048]{2,1,0:T(8,128)(2,1)} %copy.27), calls=%async_computation.2 | async-start | bytes 4194304 | tf_op jit(solution)/shard_map/all_to_all | solution.py:27
  257.9 5.5 fusion.29
  265.8 35.5 %reduce-scatter.4.cloned.1.call-done = f32[8,4,256]{2,0,1:T(8,128)} async-done(((f32[8,64,256]{2,0,1:T(8,128)}), f32[8,4,256]{2,0,1:T(8,128)}) %reduce-scatter.4.cloned.1.call-update) | async-done | bytes 32784 | tf_op jit(solution)/shard_map/reduce_scatter | solution.py:64
  302.7 69.8 %reduce-scatter.6.cloned.1.call-done = f32[8,4,256]{2,0,1:T(8,128)} async-done(((f32[8,64,256]{2,0,1:T(8,128)}), f32[8,4,256]{2,0,1:T(8,128)}) %reduce-scatter.6.cloned.1.call-update) | async-done | bytes 32784 | tf_op jit(solution)/shard_map/reduce_scatter | solution.py:65
  373.9 2.3 fusion.22
  377.2 3.6 fusion.12
  380.8 3.6 convolution_convert_fusion.2
  384.4 3.7 convolution_convert_fusion.4
  388.1 123.3 %all-reduce.3.cloned.1.call-done = f32[4,128,128]{2,0,1:T(4,128)} async-done(((f32[4,128,128]{2,0,1:T(4,128)}), f32[4,128,128]{2,0,1:T(4,128)}) %all-reduce.3.cloned.1.call-update) | async-done | bytes 262160
  512.7 71.7 %reduce-scatter.8.cloned.1.call-done = f32[4,8,128]{2,1,0:T(8,128)} async-done(((f32[4,128,128]{2,1,0:T(8,128)}), f32[4,8,128]{2,1,0:T(8,128)}) %reduce-scatter.8.cloned.1.call-update) | async-done | bytes 16400 | tf_op jit(solution)/shard_map/reduce_scatter | solution.py:66
  (37 shorter events, 11.4 us)
Async XLA Ops:
  7.2 45.8 %copy-start = (bf16[512,2048]{1,0:T(8,128)(2,1)S(1)}, bf16[512,2048]{1,0:T(8,128)(2,1)}, u32[]{:S(2)}) copy-start(bf16[512,2048]{1,0:T(8,128)(2,1)} %param.6) | copy-start | bytes 6291460
  8.9 47.8 %all-to-all-start.1 = ((bf16[16,8,4,256]{3,2,1,0:T(4,128)(2,1)}), bf16[16,8,4,256]{3,2,1,0:T(4,128)(2,1)S(1)}, u32[]{:S(2)}, u32[]{:S(2)}) async-start(bf16[16,8,4,256]{3,2,1,0:T(4,128)(2,1)} %stack.2), calls=%async_computation.1 | async-start | bytes 524288 | tf_op jit(solution)/shard_map/all_to_all | solution.py:40
  56.6 7.2 %copy-start.4 = (bf16[4,8,128]{2,1,0:T(8,128)(2,1)S(1)}, bf16[4,8,128]{2,1,0:T(8,128)(2,1)}, u32[]{:S(2)}) copy-start(bf16[4,8,128]{2,1,0:T(8,128)(2,1)} %param.11) | copy-start | bytes 24580
  56.6 62.5 %all-to-all-start = ((bf16[4,128,2048]{2,0,1:T(4,128)(2,1)}), bf16[4,128,2048]{2,0,1:T(4,128)(2,1)}, u32[]{:S(2)}, u32[]{:S(2)}) async-start(bf16[4,128,2048]{2,0,1:T(4,128)(2,1)} %copy.21), calls=%async_computation | async-start | bytes 4194304 | tf_op jit(solution)/shard_map/all_to_all | solution.py:23
  119.2 7.2 %copy-start.3 = (bf16[8,4,256]{2,1,0:T(4,128)(2,1)S(1)}, bf16[8,4,256]{2,1,0:T(4,128)(2,1)}, u32[]{:S(2)}) copy-start(bf16[8,4,256]{2,1,0:T(4,128)(2,1)} %param.9) | copy-start | bytes 49156
  119.2 66.5 %all-to-all-start.3 = ((bf16[4,128,2048]{2,0,1:T(4,128)(2,1)}), bf16[4,128,2048]{2,0,1:T(4,128)(2,1)}, u32[]{:S(2)}, u32[]{:S(2)}) async-start(bf16[4,128,2048]{2,0,1:T(4,128)(2,1)} %copy.29), calls=%async_computation.3 | async-start | bytes 4194304 | tf_op jit(solution)/shard_map/all_to_all | solution.py:23
  193.9 7.5 %copy-start.2 = (bf16[64,8,2048]{2,0,1:T(8,128)(2,1)S(1)}, bf16[64,8,2048]{2,0,1:T(8,128)(2,1)}, u32[]{:S(2)}) copy-start(bf16[64,8,2048]{2,0,1:T(8,128)(2,1)} %all_to_all.67) | copy-start | bytes 6291460
  209.9 3.2 copy-start.1
  215.7 35.4 %all-to-all-start.4 = ((bf16[64,8,2048]{2,1,0:T(8,128)(2,1)}), bf16[64,8,2048]{2,1,0:T(8,128)(2,1)}, u32[]{:S(2)}, u32[]{:S(2)}) async-start(bf16[64,8,2048]{2,1,0:T(8,128)(2,1)} %copy.33), calls=%async_computation.4 | async-start | bytes 4194304 | tf_op jit(solution)/shard_map/all_to_all | solution.py:27
  222.8 78.5 %reduce-scatter.4.cloned.1.call-start = ((), (), s32[]{:S(2)}) async-start(), calls=%async_computation.8 | async-start | bytes 557056 | tf_op jit(solution)/shard_map/reduce_scatter | solution.py:64
  251.1 126.0 %all-to-all-start.2 = ((bf16[64,8,2048]{2,1,0:T(8,128)(2,1)}), bf16[64,8,2048]{2,1,0:T(8,128)(2,1)}, u32[]{:S(2)}, u32[]{:S(2)}) async-start(bf16[64,8,2048]{2,1,0:T(8,128)(2,1)} %copy.27), calls=%async_computation.2 | async-start | bytes 4194304 | tf_op jit(solution)/shard_map/all_to_all | solution.py:27
  257.7 6.9 %copy-start.5 = (u32[256]{0:T(256)S(1)}, u32[256]{0:T(256)}, u32[]{:S(2)}) copy-start(u32[256]{0:T(256)} %constant.16) | copy-start | bytes 3076
  257.7 114.9 %reduce-scatter.6.cloned.1.call-start = ((), (), s32[]{:S(2)}) async-start(), calls=%async_computation.9 | async-start | bytes 557056 | tf_op jit(solution)/shard_map/reduce_scatter | solution.py:65
  264.5 246.9 %all-reduce.3.cloned.1.call-start = ((), (), s32[]{:S(2)}) async-start(), calls=%async_computation.11 | async-start | bytes 524288
  377.1 207.3 %reduce-scatter.8.cloned.1.call-start = ((), (), s32[]{:S(2)}) async-start(), calls=%async_computation.10 | async-start | bytes 278528 | tf_op jit(solution)/shard_map/reduce_scatter | solution.py:66
Sparse Core Ops, SparseCore 0:
  229.6 71.7 reduce-scatter.3
  304.0 68.4 reduce-scatter.5
  377.2 134.1 all-reduce.2
  514.5 69.8 reduce-scatter.7
